TPU v7x, 32 devices: a whole 2x2x4 slice. The times are simulated.
32 devices in a mesh: grp: 2 (over y), seq: 4 (over z), sub: 2 (over x), rep: 2 (over core).
Axes of the slice: x: 2, y: 2, z: 4, core: 2. Of those that a mesh axis runs over, the one named last changes fastest.
Arguments:
- inputs: bfloat16 [16, 4096, 4096], P(('grp', 'rep'), ('seq', 'sub')), parts along dimension 0, may hold values from -6 to 6
- out_grads: bfloat16 [16, 4096, 4096], P(('grp', 'rep'), ('seq', 'sub')), parts along dimension 0, may hold values from -6 to 6
- doc_lengths: int32 [16], P(('grp', 'rep')), parts along dimension 0, may hold values from 512 to 4096, as said below
- in_proj: bfloat16 [4096, 256], replicated, may hold values from -0.09375 to 0.09375
- out_proj: bfloat16 [4096, 256], replicated, may hold values from -0.09375 to 0.09375
- in_factor: float32 [256, 256], replicated, may hold values from -0.25 to 2.25, as said below
- out_factor: float32 [256, 256], replicated, may hold values from -0.25 to 2.25, as said below
- index_rows: bfloat16 [4096, 65536], P('grp', ('seq', 'sub', 'rep')), parts along dimension 0, may hold values from -0.00048828125 to 0.00048828125
Outputs:
- scores: float32 [4096, 8], P(('grp', 'seq', 'sub', 'rep')), parts along dimension 0
There are 2 independent parts, one for each index of `grp`. A program takes and returns all parts, laid end to end along the dimension named above; an argument that names none is the same for every part. Nothing has to cross between parts.
Inputs may be any that keep to these rules, and one draw needn't show every extreme that they name: `doc_lengths`: positions from a document's length on are padding. `in_factor`: symmetric. `out_factor`: symmetric.
All inputs are finite; a program needn't handle non-finite values.
Results may differ from a plain program's by a relative error of at most 0.005.
Values may be sent and summed in bfloat16 or wider, within the bound.
No kernel may reach another device: no remote copies, remote signals or barrier semaphores. Data moves between devices by JAX's collectives and lax.ppermute only.
A program may use at most 128 MiB of HBM per device.

v0:
```python
import jax
import jax.numpy as jnp
from jax import lax
from jax.sharding import PartitionSpec as P


def on_device(inputs, out_grads, doc_lengths, in_proj, out_proj, in_factor, out_factor, index_rows):
    doc_count, tok_count, model_width = inputs.shape
    rank_size = in_proj.shape[1]
    offset = lax.axis_index(("seq", "sub")) * tok_count
    positions = offset + jnp.arange(tok_count, dtype=jnp.int32)
    live = positions[None, :] < doc_lengths[:, None]
    in_rows = jnp.dot(
        inputs.reshape(-1, model_width), in_proj, preferred_element_type=jnp.float32
    ).astype(jnp.bfloat16)
    out_rows = jnp.dot(
        out_grads.reshape(-1, model_width), out_proj, preferred_element_type=jnp.float32
    ).astype(jnp.bfloat16)
    factored = jnp.dot(out_rows.astype(jnp.float32), out_factor.T, precision=lax.Precision.HIGHEST)
    factored = factored.reshape(doc_count, tok_count, rank_size) * live[:, :, None].astype(
        jnp.float32
    )
    owned_cols = lax.all_to_all(factored, ("seq", "sub"), split_axis=2, concat_axis=1, tiled=True)
    all_inputs = lax.all_gather(
        in_rows.reshape(doc_count, tok_count, rank_size), ("seq", "sub"), axis=1, tiled=True
    )
    left_grad = jnp.einsum(
        "dto,dti->doi", owned_cols, all_inputs.astype(jnp.float32), precision=lax.Precision.HIGHEST
    )
    owned_block = jnp.einsum("doi,iq->doq", left_grad, in_factor, precision=lax.Precision.HIGHEST)
    owned_sum = owned_block.reshape(doc_count, -1)
    gathered = lax.all_to_all(
        owned_sum.astype(jnp.bfloat16), "rep", split_axis=1, concat_axis=0, tiled=True
    )
    return lax.psum_scatter(
        jnp.dot(index_rows, gathered.T, preferred_element_type=jnp.float32),
        ("seq", "sub", "rep"),
        scatter_dimension=0,
        tiled=True,
    )


def solution(mesh):
    in_specs = (
        P(("grp", "rep"), ("seq", "sub"), None),
        P(("grp", "rep"), ("seq", "sub"), None),
        P(("grp", "rep")),
        P(),
        P(),
        P(),
        P(),
        P("grp", ("seq", "sub", "rep")),
    )
    out_specs = P(("grp", "seq", "sub", "rep"), None)
    return jax.shard_map(
        on_device, mesh=mesh, in_specs=in_specs, out_specs=out_specs, check_vma=False
    )
```

profile of v0, /device:TPU:0, one launch (start us, length us, event | category | flops | bytes accessed | tf_op | source)
XLA Modules:
  0.0 259.4 jit_solution(2755302112089737939)
XLA Ops:
  6.5 0.0 copy-start
  6.5 0.0 all-gather.2.cloned.1.call-start
  6.5 1.6 copy-done
  8.1 9.2 %convolution_convert_fusion = bf16[2048,256]{1,0:T(8,128)(2,1)} fusion(bf16[2048,4096]{1,0:T(8,128)(2,1)} %bitcast.37, bf16[4096,256]{1,0:T(8,128)(2,1)S(1)} %copy-done), kind=kOutput, calls=%fused_computation | convolution fusion | flops 4295491584 | bytes 19922944 | tf_op jit(solution)/shard_map/dot_general | solution.py:13
  17.3 0.0 all-gather.2.cloned.1.call-update
  17.3 0.0 reduce-scatter.2.cloned.1.call-start
  17.4 0.0 copy-start.3
  17.4 11.1 %convolution_convert_fusion.1 = bf16[2048,256]{1,0:T(8,128)(2,1)S(1)} fusion(bf16[2048,4096]{1,0:T(8,128)(2,1)} %bitcast.38, bf16[4096,256]{1,0:T(8,128)(2,1)} %param.12), kind=kOutput, calls=%fused_computation.1 | convolution fusion | flops 4295491584 | bytes 19922944 | tf_op jit(solution)/shard_map/dot_general | solution.py:16
  28.5 0.0 copy-done.3
  28.5 2.4 fusion.1
  30.9 0.0 copy-start.4
  30.9 2.2 copy.12
  33.2 0.0 copy-done.4
  33.2 0.1 compare_convert_fusion
  33.3 0.2 broadcast_multiply_fusion
  33.5 90.8 %all_to_all.34 = f32[4,512,256]{1,0,2:T(4,128)S(1)} all-to-all(f32[4,512,256]{1,0,2:T(4,128)S(1)} %bitcast.30), channel_id=1, replica_groups=mesh['grp'=2,'seq'=4,'sub'=2,'rep'=2] {'seq','sub'}, dimensions={2} | all-to-all | bytes 4194304 | tf_op jit(solution)/shard_map/all_to_all | solution.py:23
  124.3 0.7 copy.13
  125.0 0.2 copy.16
  125.2 54.7 %all-gather.2.cloned.1.call-done = bf16[4,4096,256]{2,1,0:T(8,128)(2,1)} async-done(((bf16[4,512,256]{2,1,0:T(8,128)(2,1)}), bf16[4,4096,256]{2,1,0:T(8,128)(2,1)}) %all-gather.2.cloned.1.call-update) | async-done | bytes 8388624 | tf_op jit(solution)/shard_map/all_gather | solution.py:24
  179.9 0.0 copy-start.2
  179.9 6.6 %fusion.2 = f32[4,32,256]{2,1,0:T(8,128)S(1)} fusion(f32[4,4096,32]{1,2,0:T(8,128)S(1)} %bitcast.33, bf16[4,4096,256]{2,1,0:T(8,128)(2,1)} %all-gather.2.cloned.1.call-done), kind=kOutput, calls=%fused_computation.9 | convolution fusion | flops 1610612736 | bytes 10616832 | tf_op jit(solution)/shard_map/dto,dti->doi/dot_general | solution.py:27
  186.5 0.0 copy-done.2
  186.5 0.3 convolution_convert_fusion.2
  186.8 0.1 copy.15
  186.9 4.0 %all_to_all.35 = bf16[4,2,4096]{2,0,1:T(4,128)(2,1)S(1)} all-to-all(bf16[4,2,4096]{2,0,1:T(4,128)(2,1)S(1)} %copy.15), channel_id=1, replica_groups=mesh['grp'=2,'seq'=4,'sub'=2,'rep'=2] {'rep'}, dimensions={1} | all-to-all | bytes 131072 | tf_op jit(solution)/shard_map/all_to_all | solution.py:32
  190.9 0.0 copy-start.1
  190.9 11.0 %convolution_bitcast_fusion = f32[2048,8]{0,1:T(8,128)} fusion(bf16[8,4096]{1,0:T(8,128)(2,1)S(1)} %all_to_all.31, bf16[2048,4096]{1,0:T(8,128)(2,1)} %param.15), kind=kOutput, calls=%fused_computation.2 | convolution fusion | flops 134217728 | bytes 16908288 | tf_op jit(solution)/shard_map/dot_general | solution.py:36
  201.9 0.0 reduce-scatter.2.cloned.1.call-update
  201.9 50.7 %reduce-scatter.2.cloned.1.call-done = f32[128,8]{0,1:T(8,128)} async-done(((f32[2048,8]{0,1:T(8,128)}), f32[128,8]{0,1:T(8,128)}) %reduce-scatter.2.cloned.1.call-update) | async-done | bytes 4112 | tf_op jit(solution)/shard_map/reduce_scatter | solution.py:35
  252.6 0.0 copy-done.1
  (4 shorter events, 0.1 us)
Async XLA Ops:
  6.5 1.6 copy-start
  6.5 173.4 %all-gather.2.cloned.1.call-start = ((), (), s32[]{:S(2)}) async-start(), calls=%async_computation.3 | async-start | bytes 9437184 | tf_op jit(solution)/shard_map/all_gather | solution.py:24
  17.3 235.3 %reduce-scatter.2.cloned.1.call-start = ((), (), s32[]{:S(2)}) async-start(), calls=%async_computation.4 | async-start | bytes 69632 | tf_op jit(solution)/shard_map/reduce_scatter | solution.py:35
  17.4 11.1 %copy-start.3 = (f32[256,256]{1,0:T(8,128)S(1)}, f32[256,256]{1,0:T(8,128)}, u32[]{:S(2)}) copy-start(f32[256,256]{1,0:T(8,128)} %param.14) | copy-start | bytes 786436
  30.9 2.3 copy-start.4
  179.9 6.6 %copy-start.2 = (f32[256,256]{1,0:T(8,128)S(1)}, f32[256,256]{1,0:T(8,128)}, u32[]{:S(2)}) copy-start(f32[256,256]{1,0:T(8,128)} %param.13) | copy-start | bytes 786436
  190.9 61.7 %copy-start.1 = (bf16[4096,256]{1,0:T(8,128)(2,1)S(1)}, bf16[4096,256]{1,0:T(8,128)(2,1)}, u32[]{:S(2)}) copy-start(bf16[4096,256]{1,0:T(8,128)(2,1)} %param.11) | copy-start | bytes 6291460
Sparse Core Ops, SparseCore 0:
  17.5 162.4 all-gather.1
  202.0 50.5 reduce-scatter.1
where the time goes:
time: 260 us; the launch traced here: 259 us
  waiting for transfers between devices  105 us (40%)
  blocking collectives  94.8 us (36%)
  matrix products  40.5 us (16%)
  between operations  13.5 us (5%)
  local copies, waits for them, and re-layouts  4.85 us (2%)
    all_to_all x1, blocking collectives, on_device(): lax.all_to_all(factored, ('seq', 'sub'), split_axis=2, concat_axis=1, til...  90.8 us
    all_gather x1, waiting for transfers between devices, on_device(): lax.all_gather(in_rows.reshape(doc_count, tok_count, rank_size), ('seq',...  54.7 us
    reduce_scatter x1, waiting for transfers between devices, on_device(): lax.psum_scatter(jnp.dot(index_rows, gathered.T, preferred_element_type=j...  50.7 us
    dot_general x1, matrix products, on_device(): jnp.dot(out_grads.reshape(-1, model_width), out_proj, preferred_element_t...  11.1 us
    dot_general x1, matrix products, on_device(): jnp.dot(index_rows, gathered.T, preferred_element_type=jnp.float32)  11 us
    dot_general x1, matrix products, on_device(): jnp.dot(inputs.reshape(-1, model_width), in_proj, preferred_element_type=...  9.2 us
    dot_general x1, matrix products, on_device(): jnp.einsum('dto,dti->doi', owned_cols, all_inputs.astype(jnp.float32), pr...  6.57 us
  transfers between devices with their start and end apart: 2, of which 2 were waited for; matrix products, arithmetic and copies ran while one was open for 7% of the time, Pallas kernels for 0%

commit v1 on v0

v1 whole, which is shorter than its diff:
```python
import jax
import jax.numpy as jnp
from jax import lax
from jax.sharding import PartitionSpec as P

HI = lax.Precision.HIGHEST


def on_device(inputs, out_grads, doc_lengths, in_proj, out_proj, in_factor, out_factor, index_rows):
    doc_count, tok_count, model_width = inputs.shape
    rank_size = in_proj.shape[1]
    part_size = lax.axis_size(("seq", "sub"))
    rep_size = lax.axis_size("rep")
    owner_count = part_size * rep_size
    offset = lax.axis_index(("seq", "sub")) * tok_count
    positions = offset + jnp.arange(tok_count, dtype=jnp.int32)
    live = positions[None, :] < doc_lengths[:, None]
    in_rows = jnp.dot(
        inputs.reshape(-1, model_width), in_proj, preferred_element_type=jnp.float32
    ).astype(jnp.bfloat16)
    out_rows = jnp.dot(
        out_grads.reshape(-1, model_width), out_proj, preferred_element_type=jnp.float32
    ).astype(jnp.bfloat16)
    in_rows = in_rows.reshape(doc_count, tok_count, rank_size)
    out_rows = out_rows.reshape(doc_count, tok_count, rank_size)
    out_rows = jnp.where(live[:, :, None], out_rows, jnp.zeros_like(out_rows))
    grad = jnp.einsum("dto,dti->doi", out_rows, in_rows, preferred_element_type=jnp.float32)
    left = jnp.einsum("po,doi->dpi", out_factor, grad, precision=HI)
    part = jnp.einsum("dpi,iq->dpq", left, in_factor, precision=HI).astype(jnp.bfloat16)
    part = part.reshape(doc_count, owner_count, rank_size // owner_count, rank_size)
    part = part.transpose(1, 0, 2, 3)
    got = lax.all_to_all(part, ("seq", "sub", "rep"), split_axis=0, concat_axis=0, tiled=True)
    got = got.reshape(part_size, rep_size * doc_count, -1)
    precond = jnp.sum(got.astype(jnp.float32), axis=0).astype(jnp.bfloat16)
    scores = lax.dot_general(
        precond, index_rows, (((1,), (1,)), ((), ())), preferred_element_type=jnp.float32
    )
    rows = scores.shape[1] // owner_count
    scores = scores.reshape(-1, owner_count, rows).transpose(1, 0, 2)
    mine = lax.all_to_all(scores, ("seq", "sub", "rep"), split_axis=0, concat_axis=0, tiled=True)
    return jnp.sum(mine, axis=0).T


def solution(mesh):
    in_specs = (
        P(("grp", "rep"), ("seq", "sub"), None),
        P(("grp", "rep"), ("seq", "sub"), None),
        P(("grp", "rep")),
        P(),
        P(),
        P(),
        P(),
        P("grp", ("seq", "sub", "rep")),
    )
    out_specs = P(("grp", "seq", "sub", "rep"), None)
    return jax.shard_map(
        on_device, mesh=mesh, in_specs=in_specs, out_specs=out_specs, check_vma=False
    )
```

time: 260 us -> 61.8 us (0.24)
  waiting for transfers between devices: 105 us -> 0 us
  blocking collectives: 94.8 us -> 32.3 us
  matrix products: 40.5 us -> 25.1 us
  between operations: 13.5 us -> 0.11 us
    all_to_all x2, blocking collectives: 94.8 us -> 32.3 us  [the longest x1 21.5 us: on_device(): lax.all_to_all(part, ('seq', 'sub', 'rep'), split_axis=0, concat_axis=0,...]
    all_gather x1 -> x0, waiting for transfers between devices: 54.7 us -> none  [on_device(): lax.all_gather(in_rows.reshape(doc_count, tok_count, rank_size), ('seq',...]
    reduce_scatter x1 -> x0, waiting for transfers between devices: 50.7 us -> none  [on_device(): lax.psum_scatter(jnp.dot(index_rows, gathered.T, preferred_element_type=j...]
    dot_general x4, matrix products: 20.2 us -> 11.2 us  [the longest x1 8.04 us: on_device(): lax.dot_general(precond, index_rows, (((1,), (1,)), ((), ())), preferred_...]
    dot_general x1, matrix products: 11.1 us -> 4.98 us  [on_device(): jnp.dot(out_grads.reshape(-1, model_width), out_proj, preferred_element_t...]
  transfers between devices with their start and end apart: 2 -> 0, of which waited for: 2 -> 0; matrix products, arithmetic and copies ran while one was open for 7% -> 0% of each run, Pallas kernels for 0% -> 0%
where the time goes in v1:
time: 61.8 us; the launch traced here: 61.6 us
  blocking collectives  32.3 us (52%)
  matrix products  25.1 us (41%)
  local copies, waits for them, and re-layouts  2.46 us (4%)
  other arithmetic  1.57 us (3%)
    all_to_all x1, blocking collectives, on_device(): lax.all_to_all(part, ('seq', 'sub', 'rep'), split_axis=0, concat_axis=0,...  21.5 us
    all_to_all x1, blocking collectives, on_device(): lax.all_to_all(scores, ('seq', 'sub', 'rep'), split_axis=0, concat_axis=0...  10.9 us
    dot_general x1, matrix products, on_device(): jnp.dot(inputs.reshape(-1, model_width), in_proj, preferred_element_type=...  8.95 us
    dot_general x1, matrix products, on_device(): lax.dot_general(precond, index_rows, (((1,), (1,)), ((), ())), preferred_...  8.04 us
    dot_general x1, matrix products, on_device(): jnp.dot(out_grads.reshape(-1, model_width), out_proj, preferred_element_t...  4.98 us
    unnamed x16, local copies, waits for them, and re-layouts  2.17 us

profile of v1, /device:TPU:0, one launch (start us, length us, event | category | flops | bytes accessed | tf_op | source)
XLA Modules:
  0.0 61.6 jit_solution(3428790986375526314)
XLA Ops:
  0.0 0.0 copy-start
  0.0 0.0 slice-start
  0.0 0.0 copy-start.3
  0.0 0.9 %broadcast_compare_fusion = pred[4,512]{1,0:T(4,128)(4,1)S(1)} fusion(s32[512]{0:T(512)S(1)} %iota_add_fusion, s32[4]{0:T(128)} %param.10), kind=kLoop, calls=%fused_computation.13 | loop fusion | flops 2048 | bytes 4112 | tf_op jit(solution)/shard_map/lt | solution.py:17
  0.9 0.7 %copy-done = bf16[4096,256]{1,0:T(8,128)(2,1)S(1)} copy-done((bf16[4096,256]{1,0:T(8,128)(2,1)S(1)}, bf16[4096,256]{1,0:T(8,128)(2,1)}, u32[]{:S(2)}) %copy-start) | copy-done | bytes 2097176
  1.6 0.0 slice-start.1
  1.6 0.0 slice-start.2
  1.6 0.0 slice-start.3
  1.6 9.0 %convolution_convert_fusion = bf16[2048,256]{1,0:T(8,128)(2,1)S(1)} fusion(bf16[2048,4096]{1,0:T(8,128)(2,1)} %bitcast.36, bf16[4096,256]{1,0:T(8,128)(2,1)S(1)} %copy-done), kind=kOutput, calls=%fused_computation | convolution fusion | flops 4295491584 | bytes 19922944 | tf_op jit(solution)/shard_map/dot_general | solution.py:18
  10.6 0.0 slice-done
  10.6 0.0 copy-done.3
  10.6 0.0 slice-done.1
  10.6 0.2 slice-done.2
  10.9 1.2 %slice-done.3 = s8[4194304]{0:T(1024)(128)(4,1)S(1)} async-done(((s8[16777216]{0:T(1024)(128)(4,1)}), s8[4194304]{0:T(1024)(128)(4,1)S(1)}, s32[]{:S(2)}) %slice-start.3) | async-done | bytes 4194328
  12.0 0.0 copy-start.1
  12.0 0.0 copy-start.2
  12.1 5.0 %convolution_convert_fusion.1 = bf16[2048,256]{1,0:T(8,128)(2,1)S(1)} fusion(bf16[2048,4096]{1,0:T(8,128)(2,1)S(1)} %bitcast.39, bf16[4096,256]{1,0:T(8,128)(2,1)S(1)} %copy-done.3), kind=kOutput, calls=%fused_computation.1 | convolution fusion | flops 4295491584 | bytes 19922944 | tf_op jit(solution)/shard_map/dot_general | solution.py:21
  17.0 1.1 %fusion = f32[4,256,256]{2,1,0:T(8,128)S(1)} fusion(bf16[4,512,256]{2,1,0:T(8,128)(2,1)S(1)} %bitcast.40, bf16[4,512,256]{2,1,0:T(8,128)(2,1)S(1)} %bitcast.41, pred[4,512]{1,0:T(4,128)(4,1)S(1)} %broadcast_compare_fusion), kind=kOutput, calls=%fused_computation.5 | convolution fusion | flops 268959744 | bytes 3147776 | tf_op jit(solution)/shard_map/dto,dti->doi/dot_general | solution.py:27
  18.1 0.0 copy-done.1
  18.1 1.1 %convolution_bitcast_fusion = f32[4,256,256]{2,1,0:T(8,128)S(1)} fusion(f32[4,256,256]{2,1,0:T(8,128)S(1)} %fusion, f32[256,256]{1,0:T(8,128)S(1)} %copy-done.1), kind=kOutput, calls=%fused_computation.2 | convolution fusion | flops 805306368 | bytes 2359296 | tf_op jit(solution)/shard_map/po,doi->dpi/dot_general | solution.py:28
  19.2 0.0 copy-done.2
  19.2 1.0 %convolution_convert_fusion.2 = bf16[4,256,256]{2,1,0:T(8,128)(2,1)S(1)} fusion(f32[4,256,256]{2,1,0:T(8,128)S(1)} %convolution_bitcast_fusion, f32[256,256]{1,0:T(8,128)S(1)} %copy-done.2), kind=kOutput, calls=%fused_computation.3 | convolution fusion | flops 805568512 | bytes 1835008 | tf_op jit(solution)/shard_map/dpi,iq->dpq/dot_general | solution.py:29
  20.3 21.5 %all_to_all.10 = bf16[16,4,16,256]{3,2,1,0:T(8,128)(2,1)S(1)} all-to-all(bf16[16,4,16,256]{3,2,1,0:T(8,128)(2,1)S(1)} %bitcast.35), channel_id=1, replica_groups=mesh['grp'=2,'seq'=4,'sub'=2,'rep'=2] {'seq','sub','rep'}, dimensions={0} | all-to-all | bytes 1048576 | tf_op jit(solution)/shard_map/all_to_all | solution.py:32
  41.7 0.2 reshape.57
  42.0 0.1 reduce_sum.21
  42.0 8.0 %convolution_bitcast_fusion.1 = f32[16,8,128]{2,1,0:T(8,128)S(1)} fusion(bf16[16,128,4096]{2,1,0:T(8,128)(2,1)} %bitcast.33, bf16[8,4096]{1,0:T(8,128)(2,1)S(1)} %reduce_sum.21), kind=kOutput, calls=%fused_computation.4 | convolution fusion | flops 134217728 | bytes 16908288 | tf_op jit(solution)/shard_map/dot_general | solution.py:35
  50.1 10.9 %all_to_all.11 = f32[16,8,128]{2,1,0:T(8,128)S(1)} all-to-all(f32[16,8,128]{2,1,0:T(8,128)S(1)} %convolution_bitcast_fusion.1), channel_id=1, replica_groups=mesh['grp'=2,'seq'=4,'sub'=2,'rep'=2] {'seq','sub','rep'}, dimensions={0} | all-to-all | bytes 131072 | tf_op jit(solution)/shard_map/all_to_all | solution.py:40
  61.0 0.6 reduce_sum.22
  (3 shorter events, 0.0 us)
Async XLA Ops:
  0.0 1.6 %copy-start = (bf16[4096,256]{1,0:T(8,128)(2,1)S(1)}, bf16[4096,256]{1,0:T(8,128)(2,1)}, u32[]{:S(2)}) copy-start(bf16[4096,256]{1,0:T(8,128)(2,1)} %param.11) | copy-start | bytes 6291460
  0.0 10.6 %slice-start = ((s8[16777216]{0:T(1024)(128)(4,1)}), s8[4194304]{0:T(1024)(128)(4,1)S(1)}, s32[]{:S(2)}) async-start(s8[16777216]{0:T(1024)(128)(4,1)} %bitcast.37), calls=%async_computation.2 | async-start | bytes 8388608
  0.0 10.6 %copy-start.3 = (bf16[4096,256]{1,0:T(8,128)(2,1)S(1)}, bf16[4096,256]{1,0:T(8,128)(2,1)}, u32[]{:S(2)}) copy-start(bf16[4096,256]{1,0:T(8,128)(2,1)} %param.12) | copy-start | bytes 6291460
  1.6 9.0 %slice-start.1 = ((s8[16777216]{0:T(1024)(128)(4,1)}), s8[4194304]{0:T(1024)(128)(4,1)S(1)}, s32[]{:S(2)}) async-start(s8[16777216]{0:T(1024)(128)(4,1)} %bitcast.37), calls=%async_computation.3 | async-start | bytes 8388608
  1.6 9.2 %slice-start.2 = ((s8[16777216]{0:T(1024)(128)(4,1)}), s8[4194304]{0:T(1024)(128)(4,1)S(1)}, s32[]{:S(2)}) async-start(s8[16777216]{0:T(1024)(128)(4,1)} %bitcast.37), calls=%async_computation.4 | async-start | bytes 8388608
  1.6 10.4 %slice-start.3 = ((s8[16777216]{0:T(1024)(128)(4,1)}), s8[4194304]{0:T(1024)(128)(4,1)S(1)}, s32[]{:S(2)}) async-start(s8[16777216]{0:T(1024)(128)(4,1)} %bitcast.37), calls=%async_computation.5 | async-start | bytes 8388608
  12.0 6.0 %copy-start.1 = (f32[256,256]{1,0:T(8,128)S(1)}, f32[256,256]{1,0:T(8,128)}, u32[]{:S(2)}) copy-start(f32[256,256]{1,0:T(8,128)} %param.14) | copy-start | bytes 786436
  12.0 7.2 %copy-start.2 = (f32[256,256]{1,0:T(8,128)S(1)}, f32[256,256]{1,0:T(8,128)}, u32[]{:S(2)}) copy-start(f32[256,256]{1,0:T(8,128)} %param.13) | copy-start | bytes 786436
